TPU v7x, 32 devices: a whole 2x2x4 slice. The times are simulated.
32 devices in a mesh: fsdp: 4 (over y, x), ctx: 4 (over z), tp: 2 (over core).
Axes of the slice: x: 2, y: 2, z: 4, core: 2. Of those that a mesh axis runs over, the one named last changes fastest.
Arguments:
- tokens: bfloat16 [4, 2048, 1024], P('fsdp', 'ctx'), may hold values from -6 to 6
- segment_ids: int32 [4, 2048], P('fsdp', 'ctx'), may hold values from 0 to 10, as said below
- positions: int32 [4, 2048], P('fsdp', 'ctx'), may hold values from 0 to 2047, as said below
- attention_gain: bfloat16 [1024], P('fsdp'), may hold values from 0.099609375 to 1.8984375
- attention_shift: bfloat16 [1024], P('fsdp'), may hold values from -1.75 to 1.75
- feedforward_gain: bfloat16 [1024], P('fsdp'), may hold values from 0.099609375 to 1.8984375
- feedforward_shift: bfloat16 [1024], P('fsdp'), may hold values from -1.75 to 1.75
- joint_weight: bfloat16 [1024, 3, 1024], P('fsdp', None, 'tp'), may hold values from -8 to 8
- joint_bias: bfloat16 [3, 1024], P(None, ('tp', 'fsdp')), may hold values from -3 to 3
- output_weight: bfloat16 [1024, 1024], P('tp', 'fsdp'), may hold values from -1.5 to 1.5
- output_bias: bfloat16 [1024], P('fsdp'), may hold values from -1.75 to 1.75
- up_weight: bfloat16 [1024, 4096], P('fsdp', 'tp'), may hold values from -0.1875 to 0.1875
- up_bias: bfloat16 [4096], P(('tp', 'fsdp')), may hold values from -3 to 3
- down_weight: bfloat16 [4096, 1024], P('tp', 'fsdp'), may hold values from -0.09375 to 0.09375
- down_bias: bfloat16 [1024], P('fsdp'), may hold values from -1.75 to 1.75
- cotangent: float32 [4, 2048, 1024], P('fsdp', 'ctx'), may hold values from -6 to 6
Outputs:
- result: float32 [4, 2048, 1024], P('fsdp', 'ctx')
- tokens_grad: float32 [4, 2048, 1024], P('fsdp', 'ctx')
- attention_gain_grad: float32 [1024], P('fsdp')
- attention_shift_grad: float32 [1024], P('fsdp')
- feedforward_gain_grad: float32 [1024], P('fsdp')
- feedforward_shift_grad: float32 [1024], P('fsdp')
- joint_weight_grad: float32 [1024, 3, 1024], P('fsdp', None, 'tp')
- joint_bias_grad: float32 [3, 1024], P(None, ('tp', 'fsdp'))
- output_weight_grad: float32 [1024, 1024], P('tp', 'fsdp')
- output_bias_grad: float32 [1024], P('fsdp')
- up_weight_grad: float32 [1024, 4096], P('fsdp', 'tp')
- up_bias_grad: float32 [4096], P(('tp', 'fsdp'))
- down_weight_grad: float32 [4096, 1024], P('tp', 'fsdp')
- down_bias_grad: float32 [1024], P('fsdp')
Inputs may be any that keep to these rules, and one draw needn't show every extreme that they name: `segment_ids`: along each sequence the ids start at 0 and rise by one at each document's first token; a document holds 204 to 2048 tokens, the last one cut at the sequence's end. The first sequence is one document; the last sequence is documents of 204 tokens. `positions`: each token's offset from the first token of its document; the first sequence is one document.
All inputs are finite; a program needn't handle non-finite values.
Results may differ from a plain program's by a relative error of at most 0.011.
Values may be sent and summed in bfloat16 or wider, within the bound.
No kernel may reach another device: no remote copies, remote signals or barrier semaphores. Data moves between devices by JAX's collectives and lax.ppermute only.
A program may use at most 192 MiB of HBM per device.

v0:
```python
import jax
import jax.numpy as jnp
from jax import lax
from jax.sharding import PartitionSpec as P

HD = 64
ROT = 16
EPS = 1e-05
ROPE_BASE = 10000.0


def rope_tables(offsets):
    half_dim = ROT // 2
    freq = ROPE_BASE ** (-(jnp.arange(half_dim, dtype=jnp.float32) * 2.0 / ROT))
    angle = offsets.astype(jnp.float32)[:, None] * freq[None, :]
    return (jnp.cos(angle)[:, None, :], jnp.sin(angle)[:, None, :])


def rotate(tensor, cosine, sine):
    half_dim = ROT // 2
    front = tensor[..., :half_dim]
    middle = tensor[..., half_dim:ROT]
    return jnp.concatenate(
        [front * cosine - middle * sine, middle * cosine + front * sine, tensor[..., ROT:]], axis=-1
    )


def unrotate(grads, cosine, sine):
    half_dim = ROT // 2
    front = grads[..., :half_dim]
    middle = grads[..., half_dim:ROT]
    return jnp.concatenate(
        [front * cosine + middle * sine, middle * cosine - front * sine, grads[..., ROT:]], axis=-1
    )


def normalize(rows):
    center = jnp.mean(rows, -1, keepdims=True)
    centred = rows - center
    spread = jnp.mean(centred * centred, -1, keepdims=True)
    rstd = lax.rsqrt(spread + EPS)
    return (centred * rstd, rstd)


def norm_back(upstream, normed, rstd, gain):
    scaled = upstream * gain
    return rstd * (
        scaled
        - jnp.mean(scaled, -1, keepdims=True)
        - normed * jnp.mean(scaled * normed, -1, keepdims=True)
    )


def masked_scores(query_blk, query_index, query_seg, keys, key_seg):
    scores = jnp.einsum(
        "qhe,khe->hqk", query_blk, keys, preferred_element_type=jnp.float32
    ) * HD ** (-0.5)
    key_index = jnp.arange(keys.shape[0], dtype=jnp.int32)
    allowed = (key_seg[None, :] == query_seg[:, None]) & (
        key_index[None, :] <= query_index[:, None]
    )
    return jnp.where(allowed[None], scores, -jnp.inf)


def local(
    tokens,
    segment_ids,
    positions,
    attention_gain,
    attention_shift,
    feedforward_gain,
    feedforward_shift,
    joint_weight,
    joint_bias,
    output_weight,
    output_bias,
    up_weight,
    up_bias,
    down_weight,
    down_bias,
    cotangent,
):
    f32 = jnp.float32
    bf16 = jnp.bfloat16
    scale = HD ** (-0.5)
    small = jnp.stack(
        [
            attention_gain,
            attention_shift,
            feedforward_gain,
            feedforward_shift,
            output_bias,
            down_bias,
        ]
    )
    full_joint, full_output, full_up, full_down, full_small, full_jbias, full_upbias = (
        lax.all_gather(joint_weight, "fsdp", axis=0, tiled=True),
        lax.all_gather(output_weight, "fsdp", axis=1, tiled=True),
        lax.all_gather(up_weight, "fsdp", axis=0, tiled=True),
        lax.all_gather(down_weight, "fsdp", axis=1, tiled=True),
        lax.all_gather(small, "fsdp", axis=1, tiled=True),
        lax.all_gather(joint_bias, "fsdp", axis=1, tiled=True),
        lax.all_gather(up_bias, "fsdp", axis=0, tiled=True),
    )
    params = full_small.astype(f32)
    gain_one = params[0]
    shift_one = params[1]
    gain_two = params[2]
    shift_two = params[3]
    rows = tokens[0].astype(f32)
    count_rows = rows.shape[0]
    local_width = joint_weight.shape[2]
    heads_here = local_width // HD
    normed, rstd = normalize(rows)
    first = (normed * gain_one + shift_one).astype(bf16)
    second = (normed * gain_two + shift_two).astype(bf16)
    joint = (
        jnp.einsum("nd,dpe->npe", first, full_joint, preferred_element_type=f32)
        + full_jbias.astype(f32)[None]
    )
    cosine, sine = rope_tables(positions[0])
    queries = rotate(joint[:, 0].reshape(count_rows, heads_here, HD), cosine, sine).astype(bf16)
    keys_here = rotate(joint[:, 1].reshape(count_rows, heads_here, HD), cosine, sine).astype(bf16)
    values_here = joint[:, 2].reshape(count_rows, heads_here, HD).astype(bf16)
    seg_here = segment_ids[0]
    all_keys, all_values, all_segs = (
        lax.all_gather(keys_here, "ctx", axis=0, tiled=True),
        lax.all_gather(values_here, "ctx", axis=0, tiled=True),
        lax.all_gather(seg_here.astype(bf16), "ctx", axis=0, tiled=True),
    )
    key_seg = all_segs.astype(f32)
    query_seg = seg_here.astype(f32)
    query_index = lax.axis_index("ctx") * count_rows + jnp.arange(count_rows, dtype=jnp.int32)
    block = min(512, count_rows)
    count_blocks = count_rows // block
    query_blocks = queries.reshape(count_blocks, block, heads_here, HD)
    index_blocks = query_index.reshape(count_blocks, block)
    seg_blocks = query_seg.reshape(count_blocks, block)

    def forward_block(args):
        query_blk, block_index, block_seg = args
        scores = masked_scores(query_blk, block_index, block_seg, all_keys, key_seg)
        top = jnp.max(scores, -1, keepdims=True)
        lse = top + jnp.log(jnp.sum(jnp.exp(scores - top), -1, keepdims=True))
        probs = jnp.exp(scores - lse).astype(bf16)
        mixed = jnp.einsum("hqk,khe->qhe", probs, all_values, preferred_element_type=f32)
        return (mixed, lse[..., 0])

    context32, lse_all = lax.map(forward_block, (query_blocks, index_blocks, seg_blocks))
    context32 = context32.reshape(count_rows, local_width)
    context = context32.astype(bf16)
    upper = jnp.dot(second, full_up, preferred_element_type=f32) + full_upbias.astype(f32)
    activated = jax.nn.gelu(upper, approximate=False).astype(bf16)
    partial_value = jnp.dot(context, full_output, preferred_element_type=f32) + jnp.dot(
        activated, full_down, preferred_element_type=f32
    )
    mixed_all = lax.psum(partial_value, "tp")
    result = rows + mixed_all + params[4] + params[5]
    back_joint, back_output, back_up, back_down = (
        lax.all_gather(joint_weight, "fsdp", axis=0, tiled=True),
        lax.all_gather(output_weight, "fsdp", axis=1, tiled=True),
        lax.all_gather(up_weight, "fsdp", axis=0, tiled=True),
        lax.all_gather(down_weight, "fsdp", axis=1, tiled=True),
    )
    cot = cotangent[0]
    cot_b = cot.astype(bf16)
    grad_output_w = jnp.dot(context.T, cot_b, preferred_element_type=f32)
    bias_sum = jnp.sum(cot, 0)
    grad_down_w = jnp.dot(activated.T, cot_b, preferred_element_type=f32)
    d_act = jnp.einsum("nd,fd->nf", cot_b, back_down, preferred_element_type=f32)
    unused, gelu_back = jax.vjp(lambda value: jax.nn.gelu(value, approximate=False), upper)
    d_upper = gelu_back(d_act)[0]
    d_upper_b = d_upper.astype(bf16)
    grad_up_w = jnp.dot(second.T, d_upper_b, preferred_element_type=f32)
    grad_up_b = jnp.sum(d_upper, 0)
    d_second_part = jnp.einsum("nf,df->nd", d_upper_b, back_up, preferred_element_type=f32)
    d_context = (
        jnp.einsum("nd,wd->nw", cot_b, back_output, preferred_element_type=f32)
        .astype(bf16)
        .reshape(count_rows, heads_here, HD)
    )
    delta = jnp.sum(d_context.astype(f32) * context32.reshape(count_rows, heads_here, HD), -1)
    dctx_blocks = d_context.reshape(count_blocks, block, heads_here, HD)

    def backward_block(args):
        query_blk, block_index, block_seg, dctx_blk, delta_blk, lse_blk = args
        scores = masked_scores(query_blk, block_index, block_seg, all_keys, key_seg)
        probs = jnp.exp(scores - lse_blk[..., None]).astype(bf16)
        d_probs = jnp.einsum("qhe,khe->hqk", dctx_blk, all_values, preferred_element_type=f32)
        d_scores = (probs.astype(f32) * (d_probs - jnp.transpose(delta_blk)[..., None])).astype(
            bf16
        )
        d_query_blk = (
            jnp.einsum("hqk,khe->qhe", d_scores, all_keys, preferred_element_type=f32) * scale
        )
        return (probs, d_scores, d_query_blk)

    probs_all, dscores_all, d_queries = lax.map(
        backward_block,
        (
            query_blocks,
            index_blocks,
            seg_blocks,
            dctx_blocks,
            delta.reshape(count_blocks, block, heads_here),
            lse_all,
        ),
    )
    d_queries = d_queries.reshape(count_rows, heads_here, HD)
    key_part = (
        jnp.einsum("bhqk,bqhe->khe", dscores_all, query_blocks, preferred_element_type=f32) * scale
    )
    value_part = jnp.einsum("bhqk,bqhe->khe", probs_all, dctx_blocks, preferred_element_type=f32)
    key_value = lax.psum_scatter(
        jnp.concatenate(
            [
                key_part.reshape(count_rows * lax.axis_size("ctx"), local_width),
                value_part.reshape(count_rows * lax.axis_size("ctx"), local_width),
            ],
            axis=1,
        ),
        "ctx",
        scatter_dimension=0,
        tiled=True,
    )
    d_keys = key_value[:, :local_width].reshape(count_rows, heads_here, HD)
    d_values = key_value[:, local_width:]
    d_joint = jnp.stack(
        [
            unrotate(d_queries, cosine, sine).reshape(count_rows, local_width),
            unrotate(d_keys, cosine, sine).reshape(count_rows, local_width),
            d_values,
        ],
        axis=1,
    )
    d_joint_b = d_joint.astype(bf16)
    grad_joint_w = jnp.einsum("nd,npe->dpe", first, d_joint_b, preferred_element_type=f32)
    grad_joint_b = jnp.sum(d_joint, 0)
    d_first_part = jnp.einsum("npe,dpe->nd", d_joint_b, back_joint, preferred_element_type=f32)
    d_first, d_second = lax.psum((d_first_part, d_second_part), "tp")
    norm_stats = jnp.stack(
        [
            jnp.sum(d_first * normed, 0),
            jnp.sum(d_first, 0),
            jnp.sum(d_second * normed, 0),
            jnp.sum(d_second, 0),
        ]
    )
    tokens_grad = (
        cot
        + norm_back(d_first, normed, rstd, gain_one)
        + norm_back(d_second, normed, rstd, gain_two)
    )
    grad_small = jnp.concatenate([norm_stats, bias_sum[None], bias_sum[None]], axis=0)
    share_joint, share_output, share_up, share_down, share_small, share_jbias, share_upbias = (
        lax.psum_scatter(grad_joint_w, ("fsdp", "ctx"), scatter_dimension=0, tiled=True),
        lax.psum_scatter(grad_output_w, ("fsdp", "ctx"), scatter_dimension=1, tiled=True),
        lax.psum_scatter(grad_up_w, ("fsdp", "ctx"), scatter_dimension=0, tiled=True),
        lax.psum_scatter(grad_down_w, ("fsdp", "ctx"), scatter_dimension=1, tiled=True),
        lax.psum_scatter(grad_small, ("fsdp", "ctx"), scatter_dimension=1, tiled=True),
        lax.psum_scatter(grad_joint_b, ("fsdp", "ctx"), scatter_dimension=1, tiled=True),
        lax.psum_scatter(grad_up_b, ("fsdp", "ctx"), scatter_dimension=0, tiled=True),
    )
    owned = (
        lax.all_gather(share_joint, "ctx", axis=0, tiled=True),
        lax.all_gather(share_output, "ctx", axis=1, tiled=True),
        lax.all_gather(share_up, "ctx", axis=0, tiled=True),
        lax.all_gather(share_down, "ctx", axis=1, tiled=True),
        lax.all_gather(share_small, "ctx", axis=1, tiled=True),
        lax.all_gather(share_jbias, "ctx", axis=1, tiled=True),
        lax.all_gather(share_upbias, "ctx", axis=0, tiled=True),
    )
    owned_joint, owned_output, owned_up, owned_down, owned_small, owned_jbias, owned_upbias = owned
    return (
        result[None],
        tokens_grad[None],
        owned_small[0],
        owned_small[1],
        owned_small[2],
        owned_small[3],
        owned_joint,
        owned_jbias,
        owned_output,
        owned_small[4],
        owned_up,
        owned_upbias,
        owned_down,
        owned_small[5],
    )


def solution(mesh):
    placed = (
        P("fsdp", "ctx", None),
        P("fsdp", "ctx"),
        P("fsdp", "ctx"),
        P("fsdp"),
        P("fsdp"),
        P("fsdp"),
        P("fsdp"),
        P("fsdp", None, "tp"),
        P(None, ("tp", "fsdp")),
        P("tp", "fsdp"),
        P("fsdp"),
        P("fsdp", "tp"),
        P(("tp", "fsdp")),
        P("tp", "fsdp"),
        P("fsdp"),
        P("fsdp", "ctx", None),
    )
    return jax.shard_map(
        local,
        mesh=mesh,
        in_specs=placed,
        out_specs=(
            P("fsdp", "ctx", None),
            P("fsdp", "ctx", None),
            P("fsdp"),
            P("fsdp"),
            P("fsdp"),
            P("fsdp"),
            P("fsdp", None, "tp"),
            P(None, ("tp", "fsdp")),
            P("tp", "fsdp"),
            P("fsdp"),
            P("fsdp", "tp"),
            P(("tp", "fsdp")),
            P("tp", "fsdp"),
            P("fsdp"),
        ),
        check_vma=False,
    )
```

profile of v0, /device:TPU:0, one launch (start us, length us, event | category | flops | bytes accessed | tf_op | source)
XLA Modules:
  0.0 1352.6 jit_solution(17469226401049093940)
XLA Ops:
  7.3 2.4 copy.51
  10.5 1.4 convert_reduce_fusion
  12.7 9.5 all_gather.57
  22.3 8.3 all_gather.55
  31.2 26.0 %all-gather.15.cloned.1.call-done = bf16[1024,3,512]{0,2,1:T(8,128)(2,1)} async-done(((bf16[256,3,512]{0,2,1:T(8,128)(2,1)}), bf16[1024,3,512]{0,2,1:T(8,128)(2,1)}) %all-gather.15.cloned.1.call-update) | async-done | bytes 3145744 | tf_op jit(solution)/shard_map/all_gather | solution.py:97
  57.2 3.9 convolution_add_fusion
  64.1 2.1 slice.168
  67.5 11.9 all-gather
  80.6 4.9 all-gather.21.cloned.1.call-done
  85.5 2.8 fusion.75
  89.5 44.2 %all-gather.19.cloned.1.call-done = bf16[2048,8,64]{0,2,1:T(8,128)(2,1)} async-done(((bf16[512,8,64]{0,2,1:T(8,128)(2,1)}), bf16[2048,8,64]{0,2,1:T(8,128)(2,1)}) %all-gather.19.cloned.1.call-update) | async-done | bytes 2097168 | tf_op jit(solution)/shard_map/all_gather | solution.py:127
  133.6 16.0 %fusion = (f32[8,512]{1,0:T(8,128)S(1)}, f32[8,512,2048]{2,1,0:T(8,128)}) fusion(pred[512,2048]{1,0:T(8,128)(4,1)S(1)} %fusion.7, bf16[2048,8,64]{0,2,1:T(8,128)(2,1)} %all-gather.19.cloned.1.call-done, bf16[512,8,48]{0,2,1:T(8,128)(2,1)S(1)} %slice.170, bf16[512,8,8]{0,2,1:T(8,128)(2,1)} %get-tuple-element.148, bf16[512,8,8]{0,2,1:T(8,128)(2,1)} %get-tuple-element.147), kind=kOutput, calls=%fused_computation.4 | convolution fusion | flops 1100476416 | bytes 37240832 | tf_op jit(solution)/shard_map/while/body/eval_jaxpr/qhe,khe->hqk/dot_general | solution.py:55
  149.6 15.9 %exponential_reduce_fusion = f32[8,512]{1,0:T(8,128)S(1)} fusion(f32[8,512,2048]{2,1,0:T(8,128)} %get-tuple-element.176, f32[8,512]{1,0:T(8,128)S(1)} %get-tuple-element.175, pred[512,2048]{1,0:T(8,128)(4,1)S(1)} %fusion.7), kind=kLoop, calls=%fused_computation.2 | loop fusion | flops 33550336 | bytes 34635776 | tf_op jit(solution)/shard_map/while/body/eval_jaxpr/reduce_sum | solution.py:144
  165.5 4.6 copy-done
  170.1 9.4 exponential_convert_fusion
  180.3 12.4 multiply_reduce_fusion.2
  192.7 25.3 %multiply_convert_fusion = bf16[8,512,2048]{2,1,0:T(8,128)(2,1)} fusion(bf16[8,512,2048]{2,1,0:T(8,128)(2,1)} %exponential_convert_fusion, bf16[512,8,64]{0,2,1:T(8,128)(2,1)S(1)} %bitcast.212, bf16[2048,8,64]{0,2,1:T(8,128)(2,1)} %all-gather.17.cloned.1.call-done, f32[8,512]{1,0:T(8,128)S(1)} %bitcast.227), kind=kOutput, calls=%fused_computation | convolution fusion | flops 1107296256 | bytes 36192256 | tf_op jit(solution)/shard_map/while/body/eval_jaxpr/qhe,khe->hqk/dot_general | solution.py:189
  218.1 10.9 convolution_multiply_fusion
  228.9 5.4 copy.52
  234.3 10.9 fusion.82
  245.2 5.4 copy.53
  250.6 8.2 pad_maximum_fusion
  259.4 8.0 all-gather.1
  267.5 15.1 %multiply_convert_fusion.1 = (bf16[512,2048]{1,0:T(8,128)(2,1)}, f32[512,2048]{1,0:T(8,128)}, f32[512,2048]{1,0:T(8,128)}) fusion(f32[2048]{0:T(1024)S(1)} %bitcast.253, bf16[1024,2048]{1,0:T(8,128)(2,1)} %all-gather.23.cloned.1.call-done, bf16[1,512,1024]{2,1,0:T(8,128)(2,1)S(1)} %copy-done.3, f32[1024]{0:T(1024)S(1)} %bitcast.257, f32[1024]{0:T(1024)S(1)} %bitcast.234, ...), kind=kOutput, calls=%fused_computation.9 | convolution fusion | flops 2219835392 | bytes 15749120 | tf_op jit(solution)/shard_map/dot_general | solution.py:152
  282.6 5.2 all-gather.25.cloned.1.call-done
  287.8 7.4 fusion.72
  295.2 1.3 copy-done.32
  296.6 5.8 fusion.46
  302.5 7.2 fusion.73
  310.2 6.7 fusion.81
  316.9 3.7 fusion.48
  320.6 12.7 fusion.41
  333.2 2.1 slice.136
  335.3 4.2 convolution_add_fusion.1
  339.6 95.1 %reduce-scatter.12.cloned.1.call-done = f32[512,1024]{1,0:T(8,128)} async-done(((f32[2048,1024]{1,0:T(8,128)}), f32[512,1024]{1,0:T(8,128)}) %reduce-scatter.12.cloned.1.call-update) | async-done | bytes 2097168 | tf_op jit(solution)/shard_map/reduce_scatter | solution.py:214
  434.6 3.0 fusion.68
  437.7 2.5 copy.54
  442.6 2.8 pad_maximum_fusion.2
  445.4 2.6 copy.55
  448.0 2.5 copy.56
  450.5 6.0 convolution_bitcast_fusion
  457.2 6.6 fusion.55
  463.9 3.1 fusion.43
  467.1 2.1 fusion.20
  470.1 149.9 %reduce-scatter.18.cloned.1.call-done = f32[64,2048]{1,0:T(8,128)} async-done(((f32[1024,2048]{1,0:T(8,128)}), f32[64,2048]{1,0:T(8,128)}) %reduce-scatter.18.cloned.1.call-update) | async-done | bytes 524304 | tf_op jit(solution)/shard_map/reduce_scatter | solution.py:258
  620.1 182.1 %reduce-scatter.20.cloned.1.call-done = f32[2048,64]{0,1:T(8,128)} async-done(((f32[2048,1024]{0,1:T(8,128)}), f32[2048,64]{0,1:T(8,128)}) %reduce-scatter.20.cloned.1.call-update) | async-done | bytes 524304 | tf_op jit(solution)/shard_map/reduce_scatter | solution.py:259
  802.4 33.3 %all-reduce.4.cloned.1.call-done = (f32[512,1024]{1,0:T(8,128)}, f32[512,1024]{1,0:T(8,128)}, f32[512,1024]{1,0:T(8,128)}) async-done(((f32[512,1024]{1,0:T(8,128)}, f32[512,1024]{1,0:T(8,128)}, f32[512,1024]{1,0:T(8,128)}), (f32[512,1024]{1,0:T(8,128)}, f32[512,1024]{1,0:T(8,128)}, f32[512,1024]{1,0:T(8,128)})) %all-reduce.4.cloned.1.call-update) | async-done | bytes 6291472 | tf_op jit(solution)/shard_map/psum | solution.py:157
  835.7 3.4 fusion.35
  840.2 137.3 %reduce-scatter.14.cloned.1.call-done = f32[64,3,512]{2,0,1:T(8,128)} async-done(((f32[1024,3,512]{2,0,1:T(8,128)}), f32[64,3,512]{2,0,1:T(8,128)}) %reduce-scatter.14.cloned.1.call-update) | async-done | bytes 393232 | tf_op jit(solution)/shard_map/reduce_scatter | solution.py:256
  978.8 39.4 %all-reduce = f32[2048]{0:T(1024)S(1)} all-reduce(f32[2048]{0:T(1024)S(1)} %get-tuple-element.179), channel_id=9, replica_groups=mesh['fsdp'=4,'ctx'=4,'tp'=2] {'fsdp','ctx'}, use_global_device_ids=true, to_apply=%region_25.26.clone | all-reduce | flops 2048 | bytes 16384
  1018.3 7.8 all-gather.4
  1026.1 36.4 %reduce-scatter.16.cloned.1.call-done = f32[512,64]{0,1:T(8,128)} async-done(((f32[512,1024]{0,1:T(8,128)}), f32[512,64]{0,1:T(8,128)}) %reduce-scatter.16.cloned.1.call-update) | async-done | bytes 131088 | tf_op jit(solution)/shard_map/reduce_scatter | solution.py:257
  1062.5 15.7 %all_gather.68 = f32[512,256]{0,1:T(8,128)} all-gather(f32[512,64]{0,1:T(8,128)} %reduce-scatter.16.cloned.1.call-done), channel_id=1, replica_groups=mesh['fsdp'=4,'ctx'=4,'tp'=2] {'ctx'}, dimensions={1}, use_global_device_ids=true | all-gather | bytes 655360 | tf_op jit(solution)/shard_map/all_gather | solution.py:266
  1078.2 2.0 copy.61
  1080.2 57.7 %reduce-scatter.24.cloned.1.call-done = f32[32,3]{1,0:T(8,128)} async-done(((f32[512,3]{1,0:T(8,128)}), f32[32,3]{1,0:T(8,128)}) %reduce-scatter.24.cloned.1.call-update) | async-done | bytes 400
  1138.7 12.2 all-gather.3
  1151.6 30.2 %all-gather.29.cloned.1.call-done = f32[256,2048]{1,0:T(8,128)} async-done(((f32[64,2048]{1,0:T(8,128)}), f32[256,2048]{1,0:T(8,128)}) %all-gather.29.cloned.1.call-update) | async-done | bytes 2097168 | tf_op jit(solution)/shard_map/all_gather | solution.py:267
  1181.7 46.1 %all-gather.31.cloned.1.call-done = f32[2048,256]{0,1:T(8,128)} async-done(((f32[2048,64]{0,1:T(8,128)}), f32[2048,256]{0,1:T(8,128)}) %all-gather.31.cloned.1.call-update) | async-done | bytes 2097168 | tf_op jit(solution)/shard_map/all_gather | solution.py:268
  1227.8 2.9 copy.62
  1230.7 4.9 fusion.31
  1235.6 70.6 %reduce-scatter.22.cloned.1.call-done = f32[64,6]{1,0:T(8,128)} async-done(((f32[1024,6]{1,0:T(8,128)}), f32[64,6]{1,0:T(8,128)}) %reduce-scatter.22.cloned.1.call-update) | async-done | bytes 1552
  1307.1 13.4 all-gather.2
  1321.1 20.2 %all-gather.27.cloned.1.call-done = f32[256,3,512]{2,0,1:T(8,128)} async-done(((f32[64,3,512]{2,0,1:T(8,128)}), f32[256,3,512]{2,0,1:T(8,128)}) %all-gather.27.cloned.1.call-update) | async-done | bytes 1572880 | tf_op jit(solution)/shard_map/all_gather | solution.py:265
  1341.3 2.7 copy.76
  (150 shorter events, 21.8 us)
Async XLA Ops:
  7.2 4.8 copy-start.2
  7.2 5.2 copy-start.21
  7.2 5.4 copy-start.25
  7.2 5.4 copy-start.26
  7.2 5.4 copy-start.27
  7.2 5.4 copy-start.28
  7.2 5.4 copy-start.29
  7.3 5.4 copy-start.30
  7.3 5.4 copy-start.22
  7.3 49.9 %all-gather.15.cloned.1.call-start = ((), (), s32[]{:S(2)}) async-start(), calls=%async_computation.7 | async-start | bytes 3932160 | tf_op jit(solution)/shard_map/all_gather | solution.py:97
  9.7 75.8 %all-gather.21.cloned.1.call-start = ((), (), s32[]{:S(2)}) async-start(), calls=%async_computation.10 | async-start | bytes 1310720 | tf_op jit(solution)/shard_map/all_gather | solution.py:98
  10.5 123.2 %all-gather.19.cloned.1.call-start = ((), (), s32[]{:S(2)}) async-start(), calls=%async_computation.9 | async-start | bytes 2621440 | tf_op jit(solution)/shard_map/all_gather | solution.py:127
  12.5 48.8 %copy-start.10 = (f32[512,8]{0,1:T(8,128)}, f32[512,8]{0,1:T(8,128)S(1)}, u32[]{:S(2)}) copy-start(f32[512,8]{0,1:T(8,128)S(1)} %get-tuple-element.171) | copy-start | bytes 49156
  12.6 48.8 %copy-start.12 = (f32[512,8]{0,1:T(8,128)}, f32[512,8]{0,1:T(8,128)S(1)}, u32[]{:S(2)}) copy-start(f32[512,8]{0,1:T(8,128)S(1)} %get-tuple-element.172) | copy-start | bytes 49156
  31.2 29.9 %copy-start.14 = (f32[1,1024]{1,0:T(1,128)}, f32[1,1024]{1,0:T(1,128)S(1)}, u32[]{:S(2)}) copy-start(f32[1,1024]{1,0:T(1,128)S(1)} %get-tuple-element.161) | copy-start | bytes 12292
  31.2 29.9 %copy-start.18 = (f32[1,1024]{1,0:T(1,128)}, f32[1,1024]{1,0:T(1,128)S(1)}, u32[]{:S(2)}) copy-start(f32[1,1024]{1,0:T(1,128)S(1)} %get-tuple-element.162) | copy-start | bytes 12292
  61.1 2.1 copy-start.6
  61.3 1.1 copy-start.5
  61.3 6.1 copy-start.20
  61.3 24.2 %copy-start.1 = (f32[1,512,1024]{2,1,0:T(8,128)S(1)}, f32[1,512,1024]{2,1,0:T(8,128)}, u32[]{:S(2)}) copy-start(f32[1,512,1024]{2,1,0:T(8,128)} %param.31) | copy-start | bytes 6291460
  64.1 116.3 %all-gather.17.cloned.1.call-start = ((), (), s32[]{:S(2)}) async-start(), calls=%async_computation.8 | async-start | bytes 2621440 | tf_op jit(solution)/shard_map/all_gather | solution.py:128
  66.2 201.3 %all-gather.23.cloned.1.call-start = ((), (), s32[]{:S(2)}) async-start(), calls=%async_computation.11 | async-start | bytes 5242880 | tf_op jit(solution)/shard_map/all_gather | solution.py:99
  66.8 221.0 %all-gather.25.cloned.1.call-start = ((), (), s32[]{:S(2)}) async-start(), calls=%async_computation.12 | async-start | bytes 5242880 | tf_op jit(solution)/shard_map/all_gather | solution.py:100
  67.4 367.3 %reduce-scatter.12.cloned.1.call-start = ((), (), s32[]{:S(2)}) async-start(), calls=%async_computation.13 | async-start | bytes 10485760 | tf_op jit(solution)/shard_map/reduce_scatter | solution.py:214
  149.6 20.5 %copy-start = (f32[8,512,2048]{2,1,0:T(8,128)S(1)}, f32[8,512,2048]{2,1,0:T(8,128)}, u32[]{:S(2)}) copy-start(f32[8,512,2048]{2,1,0:T(8,128)} %get-tuple-element.176) | copy-start | bytes 100663296
  179.5 13.3 copy-start.4
  192.7 25.3 %copy-start.8 = (bf16[512,8,8]{0,2,1:T(8,128)(2,1)S(1)}, bf16[512,8,8]{0,2,1:T(8,128)(2,1)}, u32[]{:S(2)}) copy-start(bf16[512,8,8]{0,2,1:T(8,128)(2,1)} %get-tuple-element.147) | copy-start | bytes 196612
  192.7 25.3 %copy-start.9 = (bf16[512,8,8]{0,2,1:T(8,128)(2,1)S(1)}, bf16[512,8,8]{0,2,1:T(8,128)(2,1)}, u32[]{:S(2)}) copy-start(bf16[512,8,8]{0,2,1:T(8,128)(2,1)} %get-tuple-element.148) | copy-start | bytes 196612
  258.7 0.7 copy-start.23
  258.7 8.8 copy-start.3
  258.8 361.2 %reduce-scatter.18.cloned.1.call-start = ((), (), s32[]{:S(2)}) async-start(), calls=%async_computation.17 | async-start | bytes 8912896 | tf_op jit(solution)/shard_map/reduce_scatter | solution.py:258
  295.2 1.3 copy-start.32
  302.4 499.7 %reduce-scatter.20.cloned.1.call-start = ((), (), s32[]{:S(2)}) async-start(), calls=%async_computation.19 | async-start | bytes 8912896 | tf_op jit(solution)/shard_map/reduce_scatter | solution.py:259
  309.7 526.0 %all-reduce.4.cloned.1.call-start = ((), (), s32[]{:S(2)}) async-start(), calls=%async_computation.23 | async-start | bytes 12582912 | tf_op jit(solution)/shard_map/psum | solution.py:157
  310.2 6.7 copy-start.24
  310.2 6.7 copy-start.33
  339.6 101.9 %copy-start.11 = (f32[512,8]{0,1:T(8,128)S(1)}, f32[512,8]{0,1:T(8,128)}, u32[]{:S(2)}) copy-start(f32[512,8]{0,1:T(8,128)} %copy-done.10) | copy-start | bytes 49156
  339.6 101.9 %copy-start.13 = (f32[512,8]{0,1:T(8,128)S(1)}, f32[512,8]{0,1:T(8,128)}, u32[]{:S(2)}) copy-start(f32[512,8]{0,1:T(8,128)} %copy-done.12) | copy-start | bytes 49156
  456.5 0.7 copy-start.15
  456.5 0.7 copy-start.19
  456.6 520.9 %reduce-scatter.14.cloned.1.call-start = ((), (), s32[]{:S(2)}) async-start(), calls=%async_computation.14 | async-start | bytes 6684672 | tf_op jit(solution)/shard_map/reduce_scatter | solution.py:256
  463.8 598.7 %reduce-scatter.16.cloned.1.call-start = ((), (), s32[]{:S(2)}) async-start(), calls=%async_computation.16 | async-start | bytes 2228224 | tf_op jit(solution)/shard_map/reduce_scatter | solution.py:257
  467.0 670.9 %reduce-scatter.24.cloned.1.call-start = ((), (), s32[]{:S(2)}) async-start(), calls=%async_computation.22 | async-start | bytes 278528
  470.0 711.7 %all-gather.29.cloned.1.call-start = ((), (), s32[]{:S(2)}) async-start(), calls=%async_computation.18 | async-start | bytes 2621440 | tf_op jit(solution)/shard_map/all_gather | solution.py:267
  620.0 607.8 %all-gather.31.cloned.1.call-start = ((), (), s32[]{:S(2)}) async-start(), calls=%async_computation.20 | async-start | bytes 2621440 | tf_op jit(solution)/shard_map/all_gather | solution.py:268
  802.2 175.4 %copy-start.31 = (u32[32]{0:T(128)S(1)}, u32[32]{0:T(128)}, u32[]{:S(2)}) copy-start(u32[32]{0:T(128)} %constant.141) | copy-start | bytes 388
  802.2 504.0 %reduce-scatter.22.cloned.1.call-start = ((), (), s32[]{:S(2)}) async-start(), calls=%async_computation.21 | async-start | bytes 557056
  839.1 391.6 %copy-start.16 = (f32[1,1024]{1,0:T(1,128)S(1)}, f32[1,1024]{1,0:T(1,128)}, u32[]{:S(2)}) copy-start(f32[1,1024]{1,0:T(1,128)} %get-tuple-element.159) | copy-start | bytes 12292
  839.1 391.6 %copy-start.17 = (f32[1,1024]{1,0:T(1,128)S(1)}, f32[1,1024]{1,0:T(1,128)}, u32[]{:S(2)}) copy-start(f32[1,1024]{1,0:T(1,128)} %get-tuple-element.160) | copy-start | bytes 12292
  840.2 501.1 %all-gather.27.cloned.1.call-start = ((), (), s32[]{:S(2)}) async-start(), calls=%async_computation.15 | async-start | bytes 1966080 | tf_op jit(solution)/shard_map/all_gather | solution.py:265
  1235.6 108.4 %copy-start.7 = (f32[256,2048]{1,0:T(8,128)S(1)}, f32[256,2048]{1,0:T(8,128)}, u32[]{:S(2)}) copy-start(f32[256,2048]{1,0:T(8,128)} %all-gather.29.cloned.1.call-done) | copy-start | bytes 6291460
Sparse Core Ops, SparseCore 0:
  10.5 46.6 all-gather.14
  59.0 26.4 all-gather.20
  87.7 45.9 all-gather.18
  135.6 44.6 all-gather.16
  182.0 51.4 all-gather.22
  235.2 52.6 all-gather.24
  290.2 144.4 reduce-scatter.11
  436.9 183.0 reduce-scatter.17
  622.3 179.8 reduce-scatter.19
  805.9 29.7 all-reduce.3
  838.1 139.3 reduce-scatter.13
  980.3 82.1 reduce-scatter.15
  1064.8 73.0 reduce-scatter.23
  1139.3 42.3 all-gather.28
  1183.1 44.6 all-gather.30
  1230.5 75.7 reduce-scatter.21
  1307.7 33.5 all-gather.26
where the time goes:
time: 1360 us; the launch traced here: 1350 us
  waiting for transfers between devices  942 us (69%)
  matrix products  161 us (12%)
  blocking collectives  126 us (9%)
  local copies, waits for them, and re-layouts  54.5 us (4%)
  other arithmetic  52.6 us (4%)
  between operations  15.4 us (1%)
    reduce_scatter x1, waiting for transfers between devices, local(): lax.psum_scatter(grad_down_w, ('fsdp', 'ctx'), scatter_dimension=1, tiled...  182 us
    reduce_scatter x1, waiting for transfers between devices, local(): lax.psum_scatter(grad_up_w, ('fsdp', 'ctx'), scatter_dimension=0, tiled=T...  150 us
    reduce_scatter x1, waiting for transfers between devices, local(): lax.psum_scatter(grad_joint_w, ('fsdp', 'ctx'), scatter_dimension=0, tile...  137 us
    unnamed x19, waiting for transfers between devices  130 us
    reduce_scatter x1, waiting for transfers between devices, local(): lax.psum_scatter(jnp.concatenate([key_part.reshape(count_rows * lax.axis_...  95.1 us
    all_gather x1, waiting for transfers between devices, local(): lax.all_gather(share_down, 'ctx', axis=1, tiled=True)  46.1 us
    all_gather x1, waiting for transfers between devices, local(): lax.all_gather(keys_here, 'ctx', axis=0, tiled=True)  44.2 us
    unnamed x1, blocking collectives  39.4 us
  transfers between devices with their start and end apart: 17, of which 16 were waited for; matrix products, arithmetic and copies ran while one was open for 19% of the time, Pallas kernels for 0%

commit v1 on v0

--- a/solution.py
+++ b/solution.py
@@ -7,6 +7,19 @@
 ROT = 16
 EPS = 1e-05
 ROPE_BASE = 10000.0
+
+
+def collect(x, axis, dim):
+    ways = lax.axis_size(axis)
+    up = [(d, (d + 1) % ways) for d in range(ways)]
+    down = [(d, (d - 1) % ways) for d in range(ways)]
+    earlier, later = ([x], [x])
+    for _ in range(ways // 2):
+        earlier.append(lax.ppermute(earlier[-1], axis, up))
+    for _ in range((ways - 1) // 2):
+        later.append(lax.ppermute(later[-1], axis, down))
+    line = jnp.concatenate([*earlier[::-1], *later[1:]], axis=dim)
+    return jnp.roll(line, (lax.axis_index(axis) - ways // 2) * x.shape[dim], axis=dim)
 
 
 def rope_tables(offsets):
@@ -264,7 +277,7 @@
     owned = (
         lax.all_gather(share_joint, "ctx", axis=0, tiled=True),
         lax.all_gather(share_output, "ctx", axis=1, tiled=True),
-        lax.all_gather(share_up, "ctx", axis=0, tiled=True),
+        collect(share_up, "ctx", 0),
         lax.all_gather(share_down, "ctx", axis=1, tiled=True),
         lax.all_gather(share_small, "ctx", axis=1, tiled=True),
         lax.all_gather(share_jbias, "ctx", axis=1, tiled=True),

time: 1360 us -> 1320 us (0.971)
  waiting for transfers between devices: 942 us -> 863 us
  local copies, waits for them, and re-layouts: 54.5 us -> 72.7 us
  blocking collectives: 126 us -> 143 us
    reduce_scatter x1, waiting for transfers between devices: 36.4 us -> 1.88 us  [local(): lax.psum_scatter(grad_output_w, ('fsdp', 'ctx'), scatter_dimension=1, til...]
    reduce_scatter x1, waiting for transfers between devices: 150 us -> 182 us  [local(): lax.psum_scatter(grad_up_w, ('fsdp', 'ctx'), scatter_dimension=0, tiled=T...]
    psum x1, waiting for transfers between devices: 33.3 us -> 2.5 us  [local(): mixed_all = lax.psum(partial_value, 'tp')]
    all_gather x1 -> x0, waiting for transfers between devices: 30.2 us -> none  [local(): lax.all_gather(share_up, 'ctx', axis=0, tiled=True)]
    reduce_scatter x1, waiting for transfers between devices: 182 us -> 153 us  [local(): lax.psum_scatter(grad_down_w, ('fsdp', 'ctx'), scatter_dimension=1, tiled...]
    ppermute x0 -> x3, waiting for transfers between devices: none -> 24 us  [the longest x2 22.4 us: collect(): earlier.append(lax.ppermute(earlier[-1], axis, up))]
    unnamed x1, blocking collectives: 39.4 us -> 55.4 us
    all_gather x1, waiting for transfers between devices: 46.1 us -> 30.3 us  [local(): lax.all_gather(share_down, 'ctx', axis=1, tiled=True)]
  transfers between devices with their start and end apart: 17 -> 19, of which waited for: 16 -> 16; matrix products, arithmetic and copies ran while one was open for 19% -> 21% of each run, Pallas kernels for 0% -> 0%
where the time goes in v1:
time: 1320 us; the launch traced here: 1310 us
  waiting for transfers between devices  863 us (65%)
  matrix products  159 us (12%)
  blocking collectives  143 us (11%)
  local copies, waits for them, and re-layouts  72.7 us (6%)
  other arithmetic  53.3 us (4%)
  between operations  15.4 us (1%)
    reduce_scatter x1, waiting for transfers between devices, local(): lax.psum_scatter(grad_up_w, ('fsdp', 'ctx'), scatter_dimension=0, tiled=T...  182 us
    reduce_scatter x1, waiting for transfers between devices, local(): lax.psum_scatter(grad_down_w, ('fsdp', 'ctx'), scatter_dimension=1, tiled...  153 us
    unnamed x18, waiting for transfers between devices  141 us
    reduce_scatter x1, waiting for transfers between devices, local(): lax.psum_scatter(grad_joint_w, ('fsdp', 'ctx'), scatter_dimension=0, tile...  135 us
    reduce_scatter x1, waiting for transfers between devices, local(): lax.psum_scatter(jnp.concatenate([key_part.reshape(count_rows * lax.axis_...  97.6 us
    unnamed x1, blocking collectives  55.4 us
    all_gather x1, waiting for transfers between devices, local(): lax.all_gather(keys_here, 'ctx', axis=0, tiled=True)  44.2 us
    unnamed x89, local copies, waits for them, and re-layouts  38.1 us
  transfers between devices with their start and end apart: 19, of which 16 were waited for; matrix products, arithmetic and copies ran while one was open for 21% of the time, Pallas kernels for 0%

profile of v1, /device:TPU:0, one launch (start us, length us, event | category | flops | bytes accessed | tf_op | source)
XLA Modules:
  0.0 1310.1 jit_solution(4276016261239933987)
XLA Ops:
  7.3 2.4 copy.51
  13.4 9.5 all_gather.54
  22.9 8.3 all_gather.52
  31.9 25.3 %all-gather.14.cloned.1.call-done = bf16[1024,3,512]{0,2,1:T(8,128)(2,1)} async-done(((bf16[256,3,512]{0,2,1:T(8,128)(2,1)}), bf16[1024,3,512]{0,2,1:T(8,128)(2,1)}) %all-gather.14.cloned.1.call-update) | async-done | bytes 3145744 | tf_op jit(solution)/shard_map/all_gather | solution.py:110
  57.2 3.9 convolution_add_fusion
  64.1 2.1 slice.168
  67.5 11.9 all-gather
  80.6 4.9 all-gather.20.cloned.1.call-done
  85.5 2.8 fusion.75
  89.5 44.2 %all-gather.18.cloned.1.call-done = bf16[2048,8,64]{0,2,1:T(8,128)(2,1)} async-done(((bf16[512,8,64]{0,2,1:T(8,128)(2,1)}), bf16[2048,8,64]{0,2,1:T(8,128)(2,1)}) %all-gather.18.cloned.1.call-update) | async-done | bytes 2097168 | tf_op jit(solution)/shard_map/all_gather | solution.py:140
  133.6 16.0 %fusion = (f32[8,512]{1,0:T(8,128)S(1)}, f32[8,512,2048]{2,1,0:T(8,128)}) fusion(pred[512,2048]{1,0:T(8,128)(4,1)S(1)} %fusion.7, bf16[2048,8,64]{0,2,1:T(8,128)(2,1)} %all-gather.18.cloned.1.call-done, bf16[512,8,48]{0,2,1:T(8,128)(2,1)S(1)} %slice.170, bf16[512,8,8]{0,2,1:T(8,128)(2,1)} %get-tuple-element.148, bf16[512,8,8]{0,2,1:T(8,128)(2,1)} %get-tuple-element.147), kind=kOutput, calls=%fused_computation.4 | convolution fusion | flops 1100476416 | bytes 37240832 | tf_op jit(solution)/shard_map/while/body/eval_jaxpr/qhe,khe->hqk/dot_general | solution.py:68
  149.6 15.9 %exponential_reduce_fusion = f32[8,512]{1,0:T(8,128)S(1)} fusion(f32[8,512,2048]{2,1,0:T(8,128)} %get-tuple-element.176, f32[8,512]{1,0:T(8,128)S(1)} %get-tuple-element.175, pred[512,2048]{1,0:T(8,128)(4,1)S(1)} %fusion.7), kind=kLoop, calls=%fused_computation.2 | loop fusion | flops 33550336 | bytes 34635776 | tf_op jit(solution)/shard_map/while/body/eval_jaxpr/reduce_sum | solution.py:157
  165.5 4.6 copy-done
  170.1 9.4 exponential_convert_fusion
  180.3 12.4 multiply_reduce_fusion.2
  192.7 25.7 %multiply_convert_fusion = bf16[8,512,2048]{2,1,0:T(8,128)(2,1)} fusion(bf16[8,512,2048]{2,1,0:T(8,128)(2,1)} %exponential_convert_fusion, bf16[512,8,64]{0,2,1:T(8,128)(2,1)S(1)} %bitcast.212, bf16[2048,8,64]{0,2,1:T(8,128)(2,1)} %all-gather.16.cloned.1.call-done, f32[8,512]{1,0:T(8,128)S(1)} %bitcast.227), kind=kOutput, calls=%fused_computation | convolution fusion | flops 1107296256 | bytes 36192256 | tf_op jit(solution)/shard_map/while/body/eval_jaxpr/qhe,khe->hqk/dot_general | solution.py:202
  218.5 10.9 convolution_multiply_fusion
  229.4 5.4 copy.52
  234.7 10.9 fusion.82
  245.6 5.4 copy.53
  251.0 8.2 pad_maximum_fusion
  259.8 8.1 all-gather.1
  267.9 14.7 %multiply_convert_fusion.1 = (bf16[512,2048]{1,0:T(8,128)(2,1)S(1)}, f32[512,2048]{1,0:T(8,128)}, f32[512,2048]{1,0:T(8,128)}) fusion(f32[2048]{0:T(1024)S(1)} %bitcast.253, bf16[1024,2048]{1,0:T(8,128)(2,1)} %all-gather.22.cloned.1.call-done, bf16[1,512,1024]{2,1,0:T(8,128)(2,1)S(1)} %copy-done.3, f32[1024]{0:T(1024)S(1)} %bitcast.257, ...), kind=kOutput, calls=%fused_computation.9 | convolution fusion | flops 2219835392 | bytes 15749120 | tf_op jit(solution)/shard_map/dot_general | solution.py:165
  283.9 5.7 fusion.73
  289.7 7.5 fusion.72
  298.5 5.8 fusion.46
  304.3 3.1 fusion.43
  308.0 6.6 fusion.81
  314.6 3.7 fusion.48
  318.3 12.6 fusion.41
  330.8 2.1 slice.136
  332.9 4.1 convolution_add_fusion.1
  337.1 97.6 %reduce-scatter.12.cloned.1.call-done = f32[512,1024]{1,0:T(8,128)} async-done(((f32[2048,1024]{1,0:T(8,128)}), f32[512,1024]{1,0:T(8,128)}) %reduce-scatter.12.cloned.1.call-update) | async-done | bytes 2097168 | tf_op jit(solution)/shard_map/reduce_scatter | solution.py:227
  434.6 3.0 fusion.68
  437.7 2.6 copy.54
  442.6 2.8 pad_maximum_fusion.2
  445.4 2.6 copy.55
  448.0 2.5 copy.56
  450.6 6.0 convolution_bitcast_fusion
  457.3 6.6 fusion.55
  463.9 2.1 fusion.20
  467.0 153.0 %reduce-scatter.20.cloned.1.call-done = f32[2048,64]{0,1:T(8,128)} async-done(((f32[2048,1024]{0,1:T(8,128)}), f32[2048,64]{0,1:T(8,128)}) %reduce-scatter.20.cloned.1.call-update) | async-done | bytes 524304 | tf_op jit(solution)/shard_map/reduce_scatter | solution.py:272
  620.1 182.1 %reduce-scatter.18.cloned.1.call-done = f32[64,2048]{1,0:T(8,128)} async-done(((f32[1024,2048]{1,0:T(8,128)}), f32[64,2048]{1,0:T(8,128)}) %reduce-scatter.18.cloned.1.call-update) | async-done | bytes 524304 | tf_op jit(solution)/shard_map/reduce_scatter | solution.py:271
  802.1 22.4 %collective-permute-done = f32[64,2048]{1,0:T(8,128)} collective-permute-done((f32[64,2048]{1,0:T(8,128)}, f32[64,2048]{1,0:T(8,128)}, u32[]{:S(2)}, u32[]{:S(2)}) %collective-permute-start) | collective-permute-done | bytes 524320 | tf_op jit(solution)/shard_map/ppermute | solution.py:18
  825.9 55.4 %all-reduce = f32[2048]{0:T(1024)S(1)} all-reduce(f32[2048]{0:T(1024)S(1)} %get-tuple-element.179), channel_id=9, replica_groups=mesh['fsdp'=4,'ctx'=4,'tp'=2] {'fsdp','ctx'}, use_global_device_ids=true, to_apply=%region_25.26.clone | all-reduce | flops 2048 | bytes 16384
  881.4 7.5 all-gather.4
  890.8 17.1 %all_gather.65 = f32[512,256]{0,1:T(8,128)} all-gather(f32[512,64]{0,1:T(8,128)} %reduce-scatter.16.cloned.1.call-done), channel_id=1, replica_groups=mesh['fsdp'=4,'ctx'=4,'tp'=2] {'ctx'}, dimensions={1}, use_global_device_ids=true | all-gather | bytes 655360 | tf_op jit(solution)/shard_map/all_gather | solution.py:279
  907.8 2.0 copy.61
  909.9 2.0 collective-permute-start.2
  915.7 1.9 constant_dynamic-update-slice_fusion.5
  920.9 2.0 constant_dynamic-update-slice_fusion.3
  923.0 2.5 all-reduce.4.cloned.1.call-done
  925.5 3.4 fusion.35
  931.9 135.2 %reduce-scatter.14.cloned.1.call-done = f32[64,3,512]{2,0,1:T(8,128)} async-done(((f32[1024,3,512]{2,0,1:T(8,128)}), f32[64,3,512]{2,0,1:T(8,128)}) %reduce-scatter.14.cloned.1.call-update) | async-done | bytes 393232 | tf_op jit(solution)/shard_map/reduce_scatter | solution.py:269
  1070.9 3.1 constant_dynamic-slice_fusion
  1074.1 68.8 %reduce-scatter.24.cloned.1.call-done = f32[32,3]{1,0:T(8,128)} async-done(((f32[512,3]{1,0:T(8,128)}), f32[32,3]{1,0:T(8,128)}) %reduce-scatter.24.cloned.1.call-update) | async-done | bytes 400
  1143.6 12.1 all-gather.3
  1156.4 30.3 %all-gather.28.cloned.1.call-done = f32[2048,256]{0,1:T(8,128)} async-done(((f32[2048,64]{0,1:T(8,128)}), f32[2048,256]{0,1:T(8,128)}) %all-gather.28.cloned.1.call-update) | async-done | bytes 2097168 | tf_op jit(solution)/shard_map/all_gather | solution.py:281
  1186.7 2.9 copy.62
  1189.6 4.8 fusion.31
  1194.5 70.6 %reduce-scatter.22.cloned.1.call-done = f32[64,6]{1,0:T(8,128)} async-done(((f32[1024,6]{1,0:T(8,128)}), f32[64,6]{1,0:T(8,128)}) %reduce-scatter.22.cloned.1.call-update) | async-done | bytes 1552
  1265.9 13.4 %all-gather.2 = f32[4,64,6]{1,2,0:T(8,128)S(1)} all-gather(f32[1,64,6]{1,2,0:T(8,128)S(1)} %bitcast.243), channel_id=1, replica_groups=mesh['fsdp'=4,'ctx'=4,'tp'=2] {'ctx'}, dimensions={0}, use_global_device_ids=true | all-gather | bytes 7680 | tf_op jit(solution)/shard_map/all_gather | solution.py:282
  1279.9 20.2 %all-gather.26.cloned.1.call-done = f32[256,3,512]{2,0,1:T(8,128)} async-done(((f32[64,3,512]{2,0,1:T(8,128)}), f32[256,3,512]{2,0,1:T(8,128)}) %all-gather.26.cloned.1.call-update) | async-done | bytes 1572880 | tf_op jit(solution)/shard_map/all_gather | solution.py:278
  1300.1 2.7 copy.82
  (161 shorter events, 39.9 us)
Async XLA Ops:
  7.2 5.4 copy-start.2
  7.2 6.0 copy-start.25
  7.2 6.1 copy-start.26
  7.2 6.1 copy-start.27
  7.2 6.1 copy-start.28
  7.2 6.1 copy-start.29
  7.2 6.1 copy-start.30
  7.3 6.1 copy-start.22
  7.3 49.9 %all-gather.14.cloned.1.call-start = ((), (), s32[]{:S(2)}) async-start(), calls=%async_computation.7 | async-start | bytes 3932160 | tf_op jit(solution)/shard_map/all_gather | solution.py:110
  9.7 75.8 %all-gather.20.cloned.1.call-start = ((), (), s32[]{:S(2)}) async-start(), calls=%async_computation.10 | async-start | bytes 1310720 | tf_op jit(solution)/shard_map/all_gather | solution.py:111
  10.4 123.2 %all-gather.18.cloned.1.call-start = ((), (), s32[]{:S(2)}) async-start(), calls=%async_computation.9 | async-start | bytes 2621440 | tf_op jit(solution)/shard_map/all_gather | solution.py:140
  13.2 48.2 %copy-start.11 = (f32[512,8]{0,1:T(8,128)}, f32[512,8]{0,1:T(8,128)S(1)}, u32[]{:S(2)}) copy-start(f32[512,8]{0,1:T(8,128)S(1)} %get-tuple-element.171) | copy-start | bytes 49156
  13.2 48.2 %copy-start.13 = (f32[512,8]{0,1:T(8,128)}, f32[512,8]{0,1:T(8,128)S(1)}, u32[]{:S(2)}) copy-start(f32[512,8]{0,1:T(8,128)S(1)} %get-tuple-element.172) | copy-start | bytes 49156
  31.9 29.2 %copy-start.15 = (f32[1,1024]{1,0:T(1,128)}, f32[1,1024]{1,0:T(1,128)S(1)}, u32[]{:S(2)}) copy-start(f32[1,1024]{1,0:T(1,128)S(1)} %get-tuple-element.161) | copy-start | bytes 12292
  31.9 29.2 %copy-start.19 = (f32[1,1024]{1,0:T(1,128)}, f32[1,1024]{1,0:T(1,128)S(1)}, u32[]{:S(2)}) copy-start(f32[1,1024]{1,0:T(1,128)S(1)} %get-tuple-element.162) | copy-start | bytes 12292
  61.1 2.1 copy-start.6
  61.3 1.1 copy-start.5
  61.3 6.1 copy-start.21
  61.3 24.2 %copy-start.1 = (f32[1,512,1024]{2,1,0:T(8,128)S(1)}, f32[1,512,1024]{2,1,0:T(8,128)}, u32[]{:S(2)}) copy-start(f32[1,512,1024]{2,1,0:T(8,128)} %param.31) | copy-start | bytes 6291460
  64.0 116.3 %all-gather.16.cloned.1.call-start = ((), (), s32[]{:S(2)}) async-start(), calls=%async_computation.8 | async-start | bytes 2621440 | tf_op jit(solution)/shard_map/all_gather | solution.py:141
  66.2 201.7 %all-gather.22.cloned.1.call-start = ((), (), s32[]{:S(2)}) async-start(), calls=%async_computation.11 | async-start | bytes 5242880 | tf_op jit(solution)/shard_map/all_gather | solution.py:112
  66.8 222.9 %all-gather.24.cloned.1.call-start = ((), (), s32[]{:S(2)}) async-start(), calls=%async_computation.12 | async-start | bytes 5242880 | tf_op jit(solution)/shard_map/all_gather | solution.py:113
  67.4 367.3 %reduce-scatter.12.cloned.1.call-start = ((), (), s32[]{:S(2)}) async-start(), calls=%async_computation.13 | async-start | bytes 10485760 | tf_op jit(solution)/shard_map/reduce_scatter | solution.py:227
  149.6 20.5 %copy-start = (f32[8,512,2048]{2,1,0:T(8,128)S(1)}, f32[8,512,2048]{2,1,0:T(8,128)}, u32[]{:S(2)}) copy-start(f32[8,512,2048]{2,1,0:T(8,128)} %get-tuple-element.176) | copy-start | bytes 100663296
  179.4 13.3 %copy-start.4 = (bf16[512,512]{0,1:T(8,128)(2,1)S(1)}, bf16[512,512]{0,1:T(8,128)(2,1)}, u32[]{:S(2)}) copy-start(bf16[512,512]{0,1:T(8,128)(2,1)} %fusion.75) | copy-start | bytes 1572868
  192.7 25.8 %copy-start.9 = (bf16[512,8,8]{0,2,1:T(8,128)(2,1)S(1)}, bf16[512,8,8]{0,2,1:T(8,128)(2,1)}, u32[]{:S(2)}) copy-start(bf16[512,8,8]{0,2,1:T(8,128)(2,1)} %get-tuple-element.147) | copy-start | bytes 196612
  192.7 25.8 %copy-start.10 = (bf16[512,8,8]{0,2,1:T(8,128)(2,1)S(1)}, bf16[512,8,8]{0,2,1:T(8,128)(2,1)}, u32[]{:S(2)}) copy-start(bf16[512,8,8]{0,2,1:T(8,128)(2,1)} %get-tuple-element.148) | copy-start | bytes 196612
  259.1 0.7 copy-start.23
  259.1 8.8 copy-start.3
  259.2 360.8 %reduce-scatter.20.cloned.1.call-start = ((), (), s32[]{:S(2)}) async-start(), calls=%async_computation.18 | async-start | bytes 8912896 | tf_op jit(solution)/shard_map/reduce_scatter | solution.py:272
  282.6 1.3 copy-start.8
  289.6 512.5 %reduce-scatter.18.cloned.1.call-start = ((), (), s32[]{:S(2)}) async-start(), calls=%async_computation.17 | async-start | bytes 8912896 | tf_op jit(solution)/shard_map/reduce_scatter | solution.py:271
  297.1 1.3 copy-start.32
  304.3 586.5 %reduce-scatter.16.cloned.1.call-start = ((), (), s32[]{:S(2)}) async-start(), calls=%async_computation.16 | async-start | bytes 2228224 | tf_op jit(solution)/shard_map/reduce_scatter | solution.py:270
  307.5 618.0 %all-reduce.4.cloned.1.call-start = ((), (), s32[]{:S(2)}) async-start(), calls=%async_computation.22 | async-start | bytes 12582912 | tf_op jit(solution)/shard_map/psum | solution.py:170
  307.9 6.6 copy-start.24
  307.9 6.6 copy-start.33
  337.1 104.4 %copy-start.12 = (f32[512,8]{0,1:T(8,128)S(1)}, f32[512,8]{0,1:T(8,128)}, u32[]{:S(2)}) copy-start(f32[512,8]{0,1:T(8,128)} %copy-done.11) | copy-start | bytes 49156
  337.1 104.4 %copy-start.14 = (f32[512,8]{0,1:T(8,128)S(1)}, f32[512,8]{0,1:T(8,128)}, u32[]{:S(2)}) copy-start(f32[512,8]{0,1:T(8,128)} %copy-done.13) | copy-start | bytes 49156
  456.6 0.7 copy-start.16
  456.6 0.7 copy-start.20
  456.6 610.5 %reduce-scatter.14.cloned.1.call-start = ((), (), s32[]{:S(2)}) async-start(), calls=%async_computation.14 | async-start | bytes 6684672 | tf_op jit(solution)/shard_map/reduce_scatter | solution.py:269
  463.9 360.8 %copy-start.31 = (u32[32]{0:T(128)S(1)}, u32[32]{0:T(128)}, u32[]{:S(2)}) copy-start(u32[32]{0:T(128)} %constant.168) | copy-start | bytes 388
  463.9 679.0 %reduce-scatter.24.cloned.1.call-start = ((), (), s32[]{:S(2)}) async-start(), calls=%async_computation.21 | async-start | bytes 278528
  466.9 719.8 %all-gather.28.cloned.1.call-start = ((), (), s32[]{:S(2)}) async-start(), calls=%async_computation.19 | async-start | bytes 2621440 | tf_op jit(solution)/shard_map/all_gather | solution.py:281
  620.0 645.0 %reduce-scatter.22.cloned.1.call-start = ((), (), s32[]{:S(2)}) async-start(), calls=%async_computation.20 | async-start | bytes 557056
  802.1 22.4 %collective-permute-start = (f32[64,2048]{1,0:T(8,128)}, f32[64,2048]{1,0:T(8,128)}, u32[]{:S(2)}, u32[]{:S(2)}) collective-permute-start(f32[64,2048]{1,0:T(8,128)} %reduce-scatter.18.cloned.1.call-done), channel_id=1, source_target_pairs={{0,2},{2,4},{4,6},{6,0},{1,3},{3,5},{5,7},{7,1},{8,10},{10,12},{12... | collective-permute-start | bytes 1572872 | tf_op jit(solution)/shard_map/ppermute | solution.py:18
  824.5 87.4 %collective-permute-start.1 = (f32[64,2048]{1,0:T(8,128)}, f32[64,2048]{1,0:T(8,128)}, u32[]{:S(2)}, u32[]{:S(2)}) collective-permute-start(f32[64,2048]{1,0:T(8,128)} %collective-permute-done), channel_id=1, source_target_pairs={{0,2},{2,4},{4,6},{6,0},{1,3},{3,5},{5,7},{7,1},{8,10},{10,12},{12... | collective-permute-start | bytes 1572872 | tf_op jit(solution)/shard_map/ppermute | solution.py:18
  909.9 9.4 collective-permute-start.2
  919.3 0.8 copy-start.7
  930.0 370.1 %all-gather.26.cloned.1.call-start = ((), (), s32[]{:S(2)}) async-start(), calls=%async_computation.15 | async-start | bytes 1966080 | tf_op jit(solution)/shard_map/all_gather | solution.py:278
  1070.9 118.7 %copy-start.17 = (f32[1,1024]{1,0:T(1,128)S(1)}, f32[1,1024]{1,0:T(1,128)}, u32[]{:S(2)}) copy-start(f32[1,1024]{1,0:T(1,128)} %get-tuple-element.159) | copy-start | bytes 12292
  1070.9 118.7 %copy-start.18 = (f32[1,1024]{1,0:T(1,128)S(1)}, f32[1,1024]{1,0:T(1,128)}, u32[]{:S(2)}) copy-start(f32[1,1024]{1,0:T(1,128)} %get-tuple-element.160) | copy-start | bytes 12292
Sparse Core Ops, SparseCore 0:
  10.5 46.6 all-gather.13
  59.0 26.4 all-gather.19
  87.7 45.9 all-gather.17
  135.6 44.6 all-gather.15
  182.0 51.4 all-gather.21
  235.1 52.6 all-gather.23
  290.1 144.4 reduce-scatter.11
  436.9 183.0 reduce-scatter.19
  622.3 179.8 reduce-scatter.17
  804.8 85.8 reduce-scatter.15
  894.7 30.7 all-reduce.3
  927.7 139.3 reduce-scatter.13
  1069.5 73.3 reduce-scatter.23
  1144.3 42.3 all-gather.27
  1189.4 75.6 reduce-scatter.21
  1266.6 33.4 all-gather.25
